TPU v7x, 128 devices: a whole 4x4x4 slice. The times are simulated.
128 devices in a mesh: elem: 16 (over z_hi, y, core), mode: 8 (over x, z_lo).
Axes of the slice: x: 4, y: 4, z: 4 (z_hi: 2, z_lo: 2; z = z_hi * 2 + z_lo), core: 2. Of those that a mesh axis runs over, the one named last changes fastest.
Arguments:
- iterate: float32 [480, 16384], P('mode', 'elem'), may hold values from -0.75 to 0.75
- newton_residual: float32 [480, 16384], P('mode', 'elem'), may hold values from -6 to 6
- inverse_blocks: float32 [64, 16384], P(None, 'elem'), may hold values from -0.15 to 2
- basis_values: bfloat16 [1024, 480], replicated, may hold values from -4 to 4, as said below
- triple_blocks: bfloat16 [8, 60, 20160], P('mode', None, 'elem'), may hold values from -0.375 to 0.375
- block_columns: int32 [8, 4], P('mode'), may hold values from 0 to 7, as said below
- neighbour_ids: int32 [256, 6], P('elem'), may hold values from 0 to 15, as said below
Outputs:
- correction: float32 [480, 16384], P('mode', 'elem')
- linear_residual: float32 [480, 16384], P('mode', 'elem')
Inputs may be any that keep to these rules, and one draw needn't show every extreme that they name: `neighbour_ids`: columns 0 to 3 give the neighbour across the -y, +y, -z, +z faces within the element's own block of 16 elements; columns 4 and 5 the neighbour across the -x and +x faces within the previous and the next block, cyclically. Neighbours are mutual across opposite faces. `block_columns`: row b names 4 different block columns; the first is b. `basis_values`: column 0 holds ones, the constant mode.
All inputs are finite; a program needn't handle non-finite values.
Results may differ from a plain program's by a relative error of at most 0.0039.
Values may be sent and summed in bfloat16 or wider, within the bound.
No kernel may reach another device: no remote copies, remote signals or barrier semaphores. Data moves between devices by JAX's collectives and lax.ppermute only.
A program may use at most 128 MiB of HBM per device.

v0:
```python
import math
import jax
import jax.numpy as jnp
import numpy as np
from jax import lax
from jax.sharding import PartitionSpec as P

K = 84
S = 1024
ITERS = 2
MB = 60
GROWTH = 0.5
TIME_STEP = 0.03
LIFT_SCALE = 6.0
PENALTY = 3.0
RELAX_WEIGHT = 0.8
SLAB_ENTRIES = 6291456
FACE_AXIS = (1, 1, 2, 2, 0, 0)
FACE_SIGN = (-1.0, 1.0, -1.0, 1.0, -1.0, 1.0)
FACE_OPPOSITE = (1, 0, 3, 2, 5, 4)


def padded(block, sides, width):
    for axis, dim in sides:
        count = lax.axis_size(axis)
        forward = [(i, i + 1) for i in range(count - 1)]
        forward.append((count - 1, 0))
        backward = [(target, source) for source, target in forward]
        low = lax.ppermute(
            lax.slice_in_dim(block, block.shape[dim] - width, None, axis=dim), axis, forward
        )
        high = lax.ppermute(lax.slice_in_dim(block, 0, width, axis=dim), axis, backward)
        block = jnp.concatenate([low, block, high], axis=dim)
    return block


def line_derivative():
    inward = 1.0 / math.sqrt(5.0)
    points = np.array([-1.0, -inward, inward, 1.0])
    legendre = (5.0 * points**3 - 3.0 * points) / 2.0
    matrix = np.zeros((4, 4))
    for source in range(4):
        for target in range(4):
            if source != target:
                matrix[source, target] = legendre[source] / (
                    legendre[target] * (points[source] - points[target])
                )
    matrix[0, 0] = -3.0
    matrix[3, 3] = 3.0
    return matrix


def direction_tables():
    line_matrix = line_derivative()
    identity = np.eye(4)
    singles = [
        np.kron(np.kron(line_matrix, identity), identity),
        np.kron(np.kron(identity, line_matrix), identity),
        np.kron(np.kron(identity, identity), line_matrix),
    ]
    return [np.kron(np.eye(2), single).T.astype(np.float32) for single in singles]


def face_nodes():
    layout = np.arange(64).reshape(4, 4, 4)
    return np.stack(
        [
            layout[:, 0, :].ravel(),
            layout[:, 3, :].ravel(),
            layout[:, :, 0].ravel(),
            layout[:, :, 3].ravel(),
            layout[0].ravel(),
            layout[3].ravel(),
        ]
    )


def embed_table():
    nodes_list = face_nodes()
    table_out = np.zeros((96, 64), np.float32)
    for face_index in range(6):
        for within in range(16):
            table_out[face_index * 16 + within, nodes_list[face_index, within]] = 1.0
    return table_out


def volume_derivative(field, single):
    modes_count = field.shape[0]
    paired = field.reshape(-1, 128)
    return jnp.dot(paired, single, precision=lax.Precision.HIGHEST).reshape(modes_count, -1)


def apply_inverse(field, inverse_blocks):
    modes_count = field.shape[0]
    shaped = field.reshape(modes_count, -1, 64)
    inverse = inverse_blocks.reshape(64, -1, 64)
    return jnp.einsum("mer,req->meq", shaped, inverse, precision=lax.Precision.HIGHEST).reshape(
        modes_count, -1
    )


def own_traces(values, flux_fields, face_index, axis_index):
    nodes_list = face_nodes()
    return (
        values[:, :, nodes_list[face_index]],
        flux_fields[axis_index][:, :, nodes_list[face_index]],
    )


def lift_terms(values, flux_fields, sources, near_ids, embed_matrix):
    pieces = []
    for face_index in range(6):
        own_values, own_fluxes = own_traces(values, flux_fields, face_index, FACE_AXIS[face_index])
        near_values = jnp.take(sources[face_index][0], near_ids[:, face_index], axis=1)
        near_fluxes = jnp.take(sources[face_index][1], near_ids[:, face_index], axis=1)
        pieces.append(
            LIFT_SCALE
            * (
                0.5 * FACE_SIGN[face_index] * (near_fluxes - own_fluxes)
                + PENALTY * (near_values - own_values)
            )
        )
    joined = jnp.concatenate(pieces, axis=2)
    return jnp.einsum("mef,fq->meq", joined, embed_matrix, precision=lax.Precision.HIGHEST)


def largest_divisor(number, ceiling):
    found = 1
    for candidate in range(1, ceiling + 1):
        if number % candidate == 0:
            found = candidate
    return found


def select_blocks(gathered, block_columns):
    pieces_list = [
        lax.dynamic_slice_in_dim(gathered, block_columns[0, stored] * MB, MB, 1)
        for stored in range(block_columns.shape[1])
    ]
    per_row = [jnp.concatenate(pieces_list, axis=1)]
    return jnp.stack(per_row)


def add_slab(running, blocks_piece, selected, coeff_terms, first_row):
    row_count = blocks_piece.shape[2] // K
    ceiling_rows = max(8, SLAB_ENTRIES // (3 * K * selected.shape[0] * selected.shape[3]))
    slab_rows = largest_divisor(row_count, ceiling_rows)
    spread = coeff_terms.astype(jnp.float32)

    def one_slab(slab_index, current):
        offset = slab_index * slab_rows
        picked = lax.dynamic_slice_in_dim(selected, first_row + offset, slab_rows, 2)
        expanded = (
            picked.astype(jnp.float32)[:, :, :, None, :] * spread[None, None, None, :, :]
        ).astype(jnp.bfloat16)
        expanded = expanded.reshape(picked.shape[0], 3, slab_rows * K, picked.shape[3])
        weights = lax.dynamic_slice_in_dim(blocks_piece, offset * K, slab_rows * K, 2)
        return current + jnp.einsum(
            "bil,bcln->cbin", weights, expanded, preferred_element_type=jnp.float32
        )

    return lax.fori_loop(0, row_count // slab_rows, one_slab, running)


def apply_jacobian(
    iterate_now, coeff_terms, triple_blocks, block_columns, neighbour_ids, tables, embed_matrix
):
    modes_local, nodes_count = iterate_now.shape
    gradients = jnp.stack([volume_derivative(iterate_now, single) for single in tables]).astype(
        jnp.bfloat16
    )
    gathered = lax.all_gather(gradients, "mode", axis=1, tiled=True)
    selected = select_blocks(gathered, block_columns)
    empty_sum = jnp.zeros((3, block_columns.shape[0], MB, nodes_count), jnp.float32)
    running = add_slab(
        empty_sum,
        lax.all_gather(triple_blocks, "elem", axis=2, tiled=True),
        selected,
        coeff_terms,
        jnp.int32(0) // K,
    )
    fluxes = running.astype(jnp.bfloat16).reshape(3, modes_local, nodes_count)
    values = iterate_now.reshape(modes_local, -1, 64)
    elements = values.shape[1]
    flux_fields = fluxes.astype(jnp.float32).reshape(3, modes_local, elements, 64)
    outward = jnp.stack(
        [
            jnp.stack(own_traces(values, flux_fields, 4, 0)),
            jnp.stack(own_traces(values, flux_fields, 5, 0)),
        ]
    )
    bordered = padded(outward.reshape(2, 2, modes_local, elements * 16), (("elem", 0),), 1)
    previous_side = bordered[0].reshape(2, modes_local, elements, 16)
    next_side = bordered[3].reshape(2, modes_local, elements, 16)
    sources = [
        own_traces(values, flux_fields, FACE_OPPOSITE[face_index], FACE_AXIS[face_index])
        for face_index in range(4)
    ]
    sources = sources + [(previous_side[0], previous_side[1]), (next_side[0], next_side[1])]
    lifted = lift_terms(values, flux_fields, sources, neighbour_ids, embed_matrix)
    divergence = lifted.reshape(modes_local, -1)
    for axis_index in range(3):
        divergence = divergence + volume_derivative(
            flux_fields[axis_index].reshape(modes_local, -1), tables[axis_index]
        )
    return iterate_now - TIME_STEP * divergence


def per_device(
    iterate,
    newton_residual,
    inverse_blocks,
    basis_values,
    triple_blocks,
    block_columns,
    neighbour_ids,
):
    tables = [jnp.asarray(single) for single in direction_tables()]
    embed_matrix = jnp.asarray(embed_table())
    modes_local = iterate.shape[0]
    low_state = iterate.astype(jnp.bfloat16)
    offset = lax.axis_index("mode") * modes_local
    local_basis = lax.dynamic_slice_in_dim(basis_values, offset, modes_local, 1)
    sampled = lax.psum_scatter(
        lax.dot_general(
            low_state, local_basis, (((0,), (1,)), ((), ())), preferred_element_type=jnp.float32
        ),
        "mode",
        scatter_dimension=0,
        tiled=True,
    )
    growth = jnp.exp(GROWTH * sampled)
    leading = basis_values[:, :K].astype(jnp.float32)
    node_terms = jnp.dot(growth, leading, precision=lax.Precision.HIGHEST) / S
    coeff_terms = lax.all_gather(node_terms.T.astype(jnp.bfloat16), "mode", axis=1, tiled=True)
    correction = apply_inverse(newton_residual, inverse_blocks)
    remainder = newton_residual
    for sweep_index in range(ITERS):
        applied = apply_jacobian(
            correction,
            coeff_terms,
            triple_blocks,
            block_columns,
            neighbour_ids,
            tables,
            embed_matrix,
        )
        remainder = newton_residual - applied
        correction = correction + RELAX_WEIGHT * apply_inverse(remainder, inverse_blocks)
    return (correction, remainder)


def solution(mesh):
    return jax.shard_map(
        per_device,
        mesh=mesh,
        in_specs=(
            P("mode", "elem"),
            P("mode", "elem"),
            P(None, "elem"),
            P(),
            P("mode", None, "elem"),
            P("mode", None),
            P("elem", None),
        ),
        out_specs=(P("mode", "elem"), P("mode", "elem")),
        check_vma=False,
    )
```

profile of v0, /device:TPU:34, one launch (start us, length us, event | category | flops | bytes accessed | tf_op | source)
XLA Modules:
  0.0 1195.9 jit_solution(10864782961386579404)
XLA Ops:
  42.5 49.8 %all-gather.6.cloned.1.call-done = bf16[1,60,20160]{1,0,2:T(2,128)(2,1)} async-done(((bf16[1,60,1260]{1,0,2:T(2,128)(2,1)}), bf16[1,60,20160]{1,0,2:T(2,128)(2,1)}) %all-gather.6.cloned.1.call-update) | async-done | bytes 2419216 | tf_op jit(solution)/shard_map/all_gather | solution.py:177
  92.3 20.8 %copy.469 = bf16[1,60,20160]{2,1,0:T(8,128)(2,1)} copy(bf16[1,60,20160]{1,0,2:T(2,128)(2,1)} %all-gather.6.cloned.1.call-done) | data formatting | bytes 4838400
  113.1 65.3 %all-gather.4.cloned.1.call-done = bf16[3,480,1024]{2,0,1:T(4,128)(2,1)} async-done(((bf16[3,60,1024]{2,0,1:T(4,128)(2,1)}), bf16[3,480,1024]{2,0,1:T(4,128)(2,1)}) %all-gather.4.cloned.1.call-update) | async-done | bytes 2949136 | tf_op jit(solution)/shard_map/all_gather | solution.py:172
  183.9 86.9 %reduce-scatter.2.cloned.1.call-done = f32[128,1024]{0,1:T(8,128)} async-done(((f32[1024,1024]{0,1:T(8,128)}), f32[128,1024]{0,1:T(8,128)}) %reduce-scatter.2.cloned.1.call-update) | async-done | bytes 524304 | tf_op jit(solution)/shard_map/reduce_scatter | solution.py:224
  272.3 22.7 %all_gather.14 = bf16[84,1024]{1,0:T(8,128)(2,1)S(1)} all-gather(bf16[84,128]{1,0:T(8,128)(2,1)S(1)} %fusion.9), channel_id=1, replica_groups=mesh['elem'=16,'mode'=8] {'mode'}, dimensions={1}, use_global_device_ids=true | all-gather | bytes 193536 | tf_op jit(solution)/shard_map/all_gather | solution.py:235
  295.1 332.9 %while.32 = (s32[]{:T(128)}, f32[3,1,60,1024]{3,2,0,1:T(8,128)S(1)}, bf16[1,3,240,1024]{3,2,1,0:T(8,128)(2,1)}, f32[84,1024]{1,0:T(8,128)S(1)}, bf16[1,60,20160]...) while((s32[]{:T(128)}, ...), condition=%wide.region_2.3_spmd.clone, body=%wide.region_1.2_spmd.clone.sunk | while | flops 756006912 | bytes 52363480 | solution.py:162
  296.0 9.4 multiply_convert_fusion.4
  305.5 15.8 %convert_element_type.114 = bf16[3,2016,1024]{2,1,0:T(8,128)(2,1)} reshape(bf16[3,24,84,1024]{3,2,1,0:T(8,128)(2,1)} %multiply_convert_fusion.4) | data formatting | bytes 24772608 | tf_op jit(solution)/shard_map/while/body/eval_jaxpr/convert_element_type | solution.py:155
  329.3 9.4 multiply_convert_fusion.4
  338.7 15.8 %convert_element_type.114 = bf16[3,2016,1024]{2,1,0:T(8,128)(2,1)} reshape(bf16[3,24,84,1024]{3,2,1,0:T(8,128)(2,1)} %multiply_convert_fusion.4) | data formatting | bytes 24772608 | tf_op jit(solution)/shard_map/while/body/eval_jaxpr/convert_element_type | solution.py:155
  362.6 9.4 multiply_convert_fusion.4
  372.0 15.8 %convert_element_type.114 = bf16[3,2016,1024]{2,1,0:T(8,128)(2,1)} reshape(bf16[3,24,84,1024]{3,2,1,0:T(8,128)(2,1)} %multiply_convert_fusion.4) | data formatting | bytes 24772608 | tf_op jit(solution)/shard_map/while/body/eval_jaxpr/convert_element_type | solution.py:155
  395.8 9.4 multiply_convert_fusion.4
  405.3 15.8 %convert_element_type.114 = bf16[3,2016,1024]{2,1,0:T(8,128)(2,1)} reshape(bf16[3,24,84,1024]{3,2,1,0:T(8,128)(2,1)} %multiply_convert_fusion.4) | data formatting | bytes 24772608 | tf_op jit(solution)/shard_map/while/body/eval_jaxpr/convert_element_type | solution.py:155
  429.1 9.4 multiply_convert_fusion.4
  438.6 15.8 %convert_element_type.114 = bf16[3,2016,1024]{2,1,0:T(8,128)(2,1)} reshape(bf16[3,24,84,1024]{3,2,1,0:T(8,128)(2,1)} %multiply_convert_fusion.4) | data formatting | bytes 24772608 | tf_op jit(solution)/shard_map/while/body/eval_jaxpr/convert_element_type | solution.py:155
  462.5 9.4 multiply_convert_fusion.4
  471.9 15.8 %convert_element_type.114 = bf16[3,2016,1024]{2,1,0:T(8,128)(2,1)} reshape(bf16[3,24,84,1024]{3,2,1,0:T(8,128)(2,1)} %multiply_convert_fusion.4) | data formatting | bytes 24772608 | tf_op jit(solution)/shard_map/while/body/eval_jaxpr/convert_element_type | solution.py:155
  495.7 9.4 multiply_convert_fusion.4
  505.2 15.8 %convert_element_type.114 = bf16[3,2016,1024]{2,1,0:T(8,128)(2,1)} reshape(bf16[3,24,84,1024]{3,2,1,0:T(8,128)(2,1)} %multiply_convert_fusion.4) | data formatting | bytes 24772608 | tf_op jit(solution)/shard_map/while/body/eval_jaxpr/convert_element_type | solution.py:155
  529.0 9.4 multiply_convert_fusion.4
  538.4 15.8 %convert_element_type.114 = bf16[3,2016,1024]{2,1,0:T(8,128)(2,1)} reshape(bf16[3,24,84,1024]{3,2,1,0:T(8,128)(2,1)} %multiply_convert_fusion.4) | data formatting | bytes 24772608 | tf_op jit(solution)/shard_map/while/body/eval_jaxpr/convert_element_type | solution.py:155
  562.3 9.4 multiply_convert_fusion.4
  571.8 15.8 %convert_element_type.114 = bf16[3,2016,1024]{2,1,0:T(8,128)(2,1)} reshape(bf16[3,24,84,1024]{3,2,1,0:T(8,128)(2,1)} %multiply_convert_fusion.4) | data formatting | bytes 24772608 | tf_op jit(solution)/shard_map/while/body/eval_jaxpr/convert_element_type | solution.py:155
  595.6 9.4 multiply_convert_fusion.4
  605.1 15.8 %convert_element_type.114 = bf16[3,2016,1024]{2,1,0:T(8,128)(2,1)} reshape(bf16[3,24,84,1024]{3,2,1,0:T(8,128)(2,1)} %multiply_convert_fusion.4) | data formatting | bytes 24772608 | tf_op jit(solution)/shard_map/while/body/eval_jaxpr/convert_element_type | solution.py:155
  716.7 68.9 %all-gather.8.cloned.1.call-done = bf16[3,480,1024]{2,0,1:T(4,128)(2,1)} async-done(((bf16[3,60,1024]{2,0,1:T(4,128)(2,1)}), bf16[3,480,1024]{2,0,1:T(4,128)(2,1)}) %all-gather.8.cloned.1.call-update) | async-done | bytes 2949136 | tf_op jit(solution)/shard_map/all_gather | solution.py:172
  791.1 333.3 %while.33 = (s32[]{:T(128)}, f32[3,1,60,1024]{3,2,0,1:T(8,128)S(1)}, bf16[1,3,240,1024]{3,2,1,0:T(8,128)(2,1)}, f32[84,1024]{1,0:T(8,128)S(1)}, bf16[1,60,20160]...) while((s32[]{:T(128)}, ...), condition=%wide.region_4.6_spmd.clone, body=%wide.region_3.5_spmd.clone.sunk | while | flops 756006912 | bytes 52363480 | solution.py:162
  792.4 9.4 multiply_convert_fusion.5
  801.9 15.8 %convert_element_type.116 = bf16[3,2016,1024]{2,1,0:T(8,128)(2,1)} reshape(bf16[3,24,84,1024]{3,2,1,0:T(8,128)(2,1)} %multiply_convert_fusion.5) | data formatting | bytes 24772608 | tf_op jit(solution)/shard_map/while/body/eval_jaxpr/convert_element_type | solution.py:155
  825.7 9.4 multiply_convert_fusion.5
  835.1 15.8 %convert_element_type.116 = bf16[3,2016,1024]{2,1,0:T(8,128)(2,1)} reshape(bf16[3,24,84,1024]{3,2,1,0:T(8,128)(2,1)} %multiply_convert_fusion.5) | data formatting | bytes 24772608 | tf_op jit(solution)/shard_map/while/body/eval_jaxpr/convert_element_type | solution.py:155
  859.0 9.4 multiply_convert_fusion.5
  868.4 15.8 %convert_element_type.116 = bf16[3,2016,1024]{2,1,0:T(8,128)(2,1)} reshape(bf16[3,24,84,1024]{3,2,1,0:T(8,128)(2,1)} %multiply_convert_fusion.5) | data formatting | bytes 24772608 | tf_op jit(solution)/shard_map/while/body/eval_jaxpr/convert_element_type | solution.py:155
  892.2 9.4 multiply_convert_fusion.5
  901.7 15.8 %convert_element_type.116 = bf16[3,2016,1024]{2,1,0:T(8,128)(2,1)} reshape(bf16[3,24,84,1024]{3,2,1,0:T(8,128)(2,1)} %multiply_convert_fusion.5) | data formatting | bytes 24772608 | tf_op jit(solution)/shard_map/while/body/eval_jaxpr/convert_element_type | solution.py:155
  925.5 9.4 multiply_convert_fusion.5
  935.0 15.8 %convert_element_type.116 = bf16[3,2016,1024]{2,1,0:T(8,128)(2,1)} reshape(bf16[3,24,84,1024]{3,2,1,0:T(8,128)(2,1)} %multiply_convert_fusion.5) | data formatting | bytes 24772608 | tf_op jit(solution)/shard_map/while/body/eval_jaxpr/convert_element_type | solution.py:155
  958.9 9.4 multiply_convert_fusion.5
  968.3 15.8 %convert_element_type.116 = bf16[3,2016,1024]{2,1,0:T(8,128)(2,1)} reshape(bf16[3,24,84,1024]{3,2,1,0:T(8,128)(2,1)} %multiply_convert_fusion.5) | data formatting | bytes 24772608 | tf_op jit(solution)/shard_map/while/body/eval_jaxpr/convert_element_type | solution.py:155
  992.1 9.4 multiply_convert_fusion.5
  1001.6 15.8 %convert_element_type.116 = bf16[3,2016,1024]{2,1,0:T(8,128)(2,1)} reshape(bf16[3,24,84,1024]{3,2,1,0:T(8,128)(2,1)} %multiply_convert_fusion.5) | data formatting | bytes 24772608 | tf_op jit(solution)/shard_map/while/body/eval_jaxpr/convert_element_type | solution.py:155
  1025.4 9.4 multiply_convert_fusion.5
  1034.8 15.8 %convert_element_type.116 = bf16[3,2016,1024]{2,1,0:T(8,128)(2,1)} reshape(bf16[3,24,84,1024]{3,2,1,0:T(8,128)(2,1)} %multiply_convert_fusion.5) | data formatting | bytes 24772608 | tf_op jit(solution)/shard_map/while/body/eval_jaxpr/convert_element_type | solution.py:155
  1058.7 9.4 multiply_convert_fusion.5
  1068.2 15.8 %convert_element_type.116 = bf16[3,2016,1024]{2,1,0:T(8,128)(2,1)} reshape(bf16[3,24,84,1024]{3,2,1,0:T(8,128)(2,1)} %multiply_convert_fusion.5) | data formatting | bytes 24772608 | tf_op jit(solution)/shard_map/while/body/eval_jaxpr/convert_element_type | solution.py:155
  1092.1 9.4 multiply_convert_fusion.5
  1101.5 15.8 %convert_element_type.116 = bf16[3,2016,1024]{2,1,0:T(8,128)(2,1)} reshape(bf16[3,24,84,1024]{3,2,1,0:T(8,128)(2,1)} %multiply_convert_fusion.5) | data formatting | bytes 24772608 | tf_op jit(solution)/shard_map/while/body/eval_jaxpr/convert_element_type | solution.py:155
  (437 shorter events, 358.3 us)
Async XLA Ops:
  7.2 85.1 %all-gather.6.cloned.1.call-start = ((), (), s32[]{:S(2)}) async-start(), calls=%async_computation.3 | async-start | bytes 10967040 | tf_op jit(solution)/shard_map/all_gather | solution.py:177
  9.4 169.0 %all-gather.4.cloned.1.call-start = ((), (), s32[]{:S(2)}) async-start(), calls=%async_computation.1 | async-start | bytes 4423680 | tf_op jit(solution)/shard_map/all_gather | solution.py:172
  16.3 254.5 %reduce-scatter.2.cloned.1.call-start = ((), (), s32[]{:S(2)}) async-start(), calls=%async_computation.2 | async-start | bytes 4718592 | tf_op jit(solution)/shard_map/reduce_scatter | solution.py:224
  20.0 9.9 copy-start.83
  20.1 765.5 %all-gather.8.cloned.1.call-start = ((), (), s32[]{:S(2)}) async-start(), calls=%async_computation.4 | async-start | bytes 4423680 | tf_op jit(solution)/shard_map/all_gather | solution.py:172
  26.8 603.3 %copy-start.60 = (s32[1024]{0:T(1024)}, s32[1024]{0:T(1024)S(1)}, u32[]{:S(2)}) copy-start(s32[1024]{0:T(1024)S(1)} %pad_clamp_fusion.3) | copy-start | bytes 12292
  29.1 603.0 %copy-start.59 = (s32[1024]{0:T(1024)}, s32[1024]{0:T(1024)S(1)}, u32[]{:S(2)}) copy-start(s32[1024]{0:T(1024)S(1)} %pad_clamp_fusion.5) | copy-start | bytes 12292
  30.0 11.2 copy-start
  30.0 602.7 %copy-start.62 = (s32[1024]{0:T(1024)}, s32[1024]{0:T(1024)S(1)}, u32[]{:S(2)}) copy-start(s32[1024]{0:T(1024)S(1)} %pad_clamp_fusion.7) | copy-start | bytes 12292
  33.3 605.1 %copy-start.63 = (s32[1024]{0:T(1024)}, s32[1024]{0:T(1024)S(1)}, u32[]{:S(2)}) copy-start(s32[1024]{0:T(1024)S(1)} %pad_clamp_fusion.11) | copy-start | bytes 12292
  34.1 79.0 %copy-start.4 = (f32[16,60,16]{0,1,2:T(8,128)}, f32[16,60,16]{0,1,2:T(8,128)S(1)}, u32[]{:S(2)}) copy-start(f32[16,60,16]{0,1,2:T(8,128)S(1)} %copy.475) | copy-start | bytes 184324
  34.8 634.9 %copy-start.72 = (pred[16]{0:T(512)(128)(4,1)}, pred[16]{0:T(512)(128)(4,1)S(1)}, u32[]{:S(2)}) copy-start(pred[16]{0:T(512)(128)(4,1)S(1)} %get-tuple-element.439) | copy-start | bytes 52
  34.8 637.0 %copy-start.74 = (pred[16]{0:T(512)(128)(4,1)}, pred[16]{0:T(512)(128)(4,1)S(1)}, u32[]{:S(2)}) copy-start(pred[16]{0:T(512)(128)(4,1)S(1)} %get-tuple-element.441) | copy-start | bytes 52
  34.8 647.6 %copy-start.68 = (pred[16]{0:T(512)(128)(4,1)}, pred[16]{0:T(512)(128)(4,1)S(1)}, u32[]{:S(2)}) copy-start(pred[16]{0:T(512)(128)(4,1)S(1)} %get-tuple-element.395) | copy-start | bytes 52
  34.9 649.9 %copy-start.70 = (pred[16]{0:T(512)(128)(4,1)}, pred[16]{0:T(512)(128)(4,1)S(1)}, u32[]{:S(2)}) copy-start(pred[16]{0:T(512)(128)(4,1)S(1)} %get-tuple-element.443) | copy-start | bytes 52
  34.9 610.0 %copy-start.65 = (s32[1024]{0:T(1024)}, s32[1024]{0:T(1024)S(1)}, u32[]{:S(2)}) copy-start(s32[1024]{0:T(1024)S(1)} %pad_clamp_fusion.4) | copy-start | bytes 12292
  36.3 611.2 %copy-start.64 = (s32[1024]{0:T(1024)}, s32[1024]{0:T(1024)S(1)}, u32[]{:S(2)}) copy-start(s32[1024]{0:T(1024)S(1)} %pad_clamp_fusion.6) | copy-start | bytes 12292
  38.7 611.2 %copy-start.61 = (s32[1024]{0:T(1024)}, s32[1024]{0:T(1024)S(1)}, u32[]{:S(2)}) copy-start(s32[1024]{0:T(1024)S(1)} %pad_clamp_fusion.8) | copy-start | bytes 12292
  41.1 612.1 %copy-start.66 = (s32[1024]{0:T(1024)}, s32[1024]{0:T(1024)S(1)}, u32[]{:S(2)}) copy-start(s32[1024]{0:T(1024)S(1)} %pad_clamp_fusion.10) | copy-start | bytes 12292
  632.1 9.5 copy-start.53
  632.7 10.7 copy-start.52
  642.3 31.6 %collective-permute-start.1 = (f32[1,2,60,256]{2,3,1,0:T(8,128)}, f32[1,2,60,256]{2,3,1,0:T(8,128)}, u32[]{:S(2)}, u32[]{:S(2)}) collective-permute-start(f32[1,2,60,256]{2,3,1,0:T(8,128)} %pad_maximum_fusion.3), channel_id=1, source_target_pairs={{8,0},{16,8},{24,16},{32,24},{40,32},{48,40},{56,48},{64,56},{72,6... | collective-permute-start | bytes 368648 | tf_op jit(solution)/shard_map/ppermute | solution.py:32
  644.1 17.0 %copy-start.50 = (f32[128,128]{1,0:T(8,128)S(1)}, f32[128,128]{1,0:T(8,128)}, u32[]{:S(2)}) copy-start(f32[128,128]{1,0:T(8,128)} %constant.210.clone) | copy-start | bytes 196612
  644.1 34.1 %collective-permute-start = (f32[1,2,60,256]{2,3,1,0:T(8,128)}, f32[1,2,60,256]{2,3,1,0:T(8,128)}, u32[]{:S(2)}, u32[]{:S(2)}) collective-permute-start(f32[1,2,60,256]{2,3,1,0:T(8,128)} %pad_maximum_fusion.2), channel_id=1, source_target_pairs={{0,8},{8,16},{16,24},{24,32},{32,40},{40,48},{48,56},{56,64},{64,7... | collective-permute-start | bytes 368648 | tf_op jit(solution)/shard_map/ppermute | solution.py:29
  646.2 18.5 %copy-start.3 = (f32[16,60,16]{0,1,2:T(8,128)S(1)}, f32[16,60,16]{0,1,2:T(8,128)}, u32[]{:S(2)}) copy-start(f32[16,60,16]{0,1,2:T(8,128)} %copy.483) | copy-start | bytes 184324
  646.2 18.6 %copy-start.76 = (pred[16]{0:T(512)(128)(4,1)S(1)}, pred[16]{0:T(512)(128)(4,1)}, u32[]{:S(2)}) copy-start(pred[16]{0:T(512)(128)(4,1)} %get-tuple-element.435) | copy-start | bytes 52
  649.9 14.8 %copy-start.5 = (f32[16,60,16]{0,1,2:T(8,128)}, f32[16,60,16]{0,1,2:T(8,128)S(1)}, u32[]{:S(2)}) copy-start(f32[16,60,16]{0,1,2:T(8,128)S(1)} %copy.473) | copy-start | bytes 184324
  649.9 17.4 %copy-start.1 = (f32[16,60,16]{0,1,2:T(8,128)S(1)}, f32[16,60,16]{0,1,2:T(8,128)}, u32[]{:S(2)}) copy-start(f32[16,60,16]{0,1,2:T(8,128)} %copy-done) | copy-start | bytes 184324
  649.9 17.4 %copy-start.78 = (pred[16]{0:T(512)(128)(4,1)S(1)}, pred[16]{0:T(512)(128)(4,1)}, u32[]{:S(2)}) copy-start(pred[16]{0:T(512)(128)(4,1)} %get-tuple-element.437) | copy-start | bytes 52
  673.9 8.5 copy-start.27
  704.4 8.8 copy-start.21
  706.1 8.8 copy-start.20
  708.1 79.8 %copy-start.10 = (f32[16,60,16]{0,1,2:T(8,128)}, f32[16,60,16]{0,1,2:T(8,128)S(1)}, u32[]{:S(2)}) copy-start(f32[16,60,16]{0,1,2:T(8,128)S(1)} %copy.526) | copy-start | bytes 184324
  1128.2 10.1 copy-start.54
  1134.5 16.2 %copy-start.18 = (f32[16,60,16]{1,2,0:T(8,128)S(1)}, f32[16,60,16]{1,2,0:T(8,128)}, u32[]{:S(2)}) copy-start(f32[16,60,16]{1,2,0:T(8,128)} %gather_fusion.12) | copy-start | bytes 184324
  1134.5 18.0 %copy-start.17 = (f32[16,60,16]{1,2,0:T(8,128)S(1)}, f32[16,60,16]{1,2,0:T(8,128)}, u32[]{:S(2)}) copy-start(f32[16,60,16]{1,2,0:T(8,128)} %gather_fusion.13) | copy-start | bytes 184324
  1137.2 33.4 %collective-permute-start.2 = (f32[1,2,60,256]{2,3,1,0:T(8,128)}, f32[1,2,60,256]{2,3,1,0:T(8,128)}, u32[]{:S(2)}, u32[]{:S(2)}) collective-permute-start(f32[1,2,60,256]{2,3,1,0:T(8,128)} %pad_maximum_fusion.4), channel_id=1, source_target_pairs={{0,8},{8,16},{16,24},{24,32},{32,40},{40,48},{48,56},{56,64},{64,7... | collective-permute-start | bytes 368648 | tf_op jit(solution)/shard_map/ppermute | solution.py:29
  1139.1 22.2 %copy-start.51 = (f32[128,128]{1,0:T(8,128)S(1)}, f32[128,128]{1,0:T(8,128)}, u32[]{:S(2)}) copy-start(f32[128,128]{1,0:T(8,128)} %constant.210.clone) | copy-start | bytes 196612
  1139.1 35.8 %collective-permute-start.3 = (f32[1,2,60,256]{2,3,1,0:T(8,128)}, f32[1,2,60,256]{2,3,1,0:T(8,128)}, u32[]{:S(2)}, u32[]{:S(2)}) collective-permute-start(f32[1,2,60,256]{2,3,1,0:T(8,128)} %pad_maximum_fusion.5), channel_id=1, source_target_pairs={{8,0},{16,8},{24,16},{32,24},{40,32},{48,40},{56,48},{64,56},{72,6... | collective-permute-start | bytes 368648 | tf_op jit(solution)/shard_map/ppermute | solution.py:32
  1147.1 17.6 %copy-start.11 = (f32[16,60,16]{0,1,2:T(8,128)S(1)}, f32[16,60,16]{0,1,2:T(8,128)}, u32[]{:S(2)}) copy-start(f32[16,60,16]{0,1,2:T(8,128)} %copy-done.10) | copy-start | bytes 184324
  1147.1 17.6 %copy-start.13 = (f32[16,60,16]{0,1,2:T(8,128)S(1)}, f32[16,60,16]{0,1,2:T(8,128)}, u32[]{:S(2)}) copy-start(f32[16,60,16]{0,1,2:T(8,128)} %copy-done.12) | copy-start | bytes 184324
  1147.1 17.6 %copy-start.77 = (pred[16]{0:T(512)(128)(4,1)S(1)}, pred[16]{0:T(512)(128)(4,1)}, u32[]{:S(2)}) copy-start(pred[16]{0:T(512)(128)(4,1)} %get-tuple-element.435) | copy-start | bytes 52
  1147.1 17.6 %copy-start.79 = (pred[16]{0:T(512)(128)(4,1)S(1)}, pred[16]{0:T(512)(128)(4,1)}, u32[]{:S(2)}) copy-start(pred[16]{0:T(512)(128)(4,1)} %get-tuple-element.437) | copy-start | bytes 52
  1156.1 12.0 %copy-start.73 = (pred[16]{0:T(512)(128)(4,1)S(1)}, pred[16]{0:T(512)(128)(4,1)}, u32[]{:S(2)}) copy-start(pred[16]{0:T(512)(128)(4,1)} %copy-done.72) | copy-start | bytes 52
  1156.1 12.1 %copy-start.75 = (pred[16]{0:T(512)(128)(4,1)S(1)}, pred[16]{0:T(512)(128)(4,1)}, u32[]{:S(2)}) copy-start(pred[16]{0:T(512)(128)(4,1)} %copy-done.74) | copy-start | bytes 52
  1170.6 8.5 copy-start.31
  1170.6 8.5 copy-start.69
  1170.6 8.5 copy-start.71
  (45 other events, 216.5 us)
Sparse Core Ops, SparseCore 0:
  10.5 81.7 all-gather.5
  94.0 84.4 all-gather.3
  180.8 89.9 reduce-scatter.1
  697.4 88.1 all-gather.7
where the time goes:
time: 1210 us; the launch traced here: 1200 us
  local copies, waits for them, and re-layouts  474 us (39%)
  waiting for transfers between devices  271 us (22%)
  other arithmetic  243 us (20%)
  matrix products  160 us (13%)
  blocking collectives  22.7 us (2%)
  between operations  18 us (1%)
    convert_element_type x20, local copies, waits for them, and re-layouts, one_slab(): expanded = (picked.astype(jnp.float32)[:, :, :, None, :] * spread[None, N...  315 us
    convert_element_type x20, other arithmetic, one_slab(): expanded = (picked.astype(jnp.float32)[:, :, :, None, :] * spread[None, N...  189 us
    dot_general x20, matrix products, one_slab(): jnp.einsum('bil,bcln->cbin', weights, expanded, preferred_element_type=jn...  142 us
    all_gather x2, waiting for transfers between devices, apply_jacobian(): gathered = lax.all_gather(gradients, 'mode', axis=1, tiled=True)  134 us
    reduce_scatter x1, waiting for transfers between devices, per_device(): lax.psum_scatter(lax.dot_general(low_state, local_basis, (((0,), (1,)), (...  86.9 us
    all_gather x1, waiting for transfers between devices, apply_jacobian(): lax.all_gather(triple_blocks, 'elem', axis=2, tiled=True)  49.8 us
    unnamed x174, local copies, waits for them, and re-layouts  29.8 us
  transfers between devices with their start and end apart: 8, of which 4 were waited for; matrix products, arithmetic and copies ran while one was open for 12% of the time, Pallas kernels for 0%

commit v1 on v0

--- a/solution.py
+++ b/solution.py
@@ -169,7 +169,9 @@
     gradients = jnp.stack([volume_derivative(iterate_now, single) for single in tables]).astype(
         jnp.bfloat16
     )
-    gathered = lax.all_gather(gradients, "mode", axis=1, tiled=True)
+    gathered = jnp.concatenate(
+        lax.all_to_all(jnp.stack([gradients] * lax.axis_size("mode")), "mode", 0, 0), axis=1
+    )
     selected = select_blocks(gathered, block_columns)
     empty_sum = jnp.zeros((3, block_columns.shape[0], MB, nodes_count), jnp.float32)
     running = add_slab(

time: 1210 us -> 1080 us (0.89)
  waiting for transfers between devices: 271 us -> 117 us
  starting transfers between devices: 6.18 us -> 20.3 us
    all_gather x2 -> x0, waiting for transfers between devices: 134 us -> none  [apply_jacobian(): gathered = lax.all_gather(gradients, 'mode', axis=1, tiled=True)]
    reduce_scatter x1, waiting for transfers between devices: 86.9 us -> 0.01 us  [per_device(): lax.psum_scatter(lax.dot_general(low_state, local_basis, (((0,), (1,)), (...]
    all_to_all x0 -> x2, waiting for transfers between devices: none -> 53.8 us  [apply_jacobian(): lax.all_to_all(jnp.stack([gradients] * lax.axis_size('mode')), 'mode', 0, 0)]
    reshape x0 -> x4, local copies, waits for them, and re-layouts: none -> 16.8 us  [apply_jacobian(): jnp.concatenate(lax.all_to_all(jnp.stack([gradients] * lax.axis_size('mod...]
    all_to_all x0 -> x2, starting transfers between devices: none -> 14 us  [apply_jacobian(): lax.all_to_all(jnp.stack([gradients] * lax.axis_size('mode')), 'mode', 0, 0)]
    all_gather x1, waiting for transfers between devices: 49.8 us -> 62.9 us  [apply_jacobian(): lax.all_gather(triple_blocks, 'elem', axis=2, tiled=True)]
    unnamed x174 -> x214, local copies, waits for them, and re-layouts: 29.8 us -> 26.6 us
  transfers between devices with their start and end apart: 8 -> 8, of which waited for: 4 -> 3; matrix products, arithmetic and copies ran while one was open for 12% -> 13% of each run, Pallas kernels for 0% -> 0%
where the time goes in v1:
time: 1080 us; the launch traced here: 1060 us
  local copies, waits for them, and re-layouts  481 us (45%)
  other arithmetic  236 us (22%)
  matrix products  161 us (15%)
  waiting for transfers between devices  117 us (11%)
  blocking collectives  22.8 us (2%)
  starting transfers between devices  20.3 us (2%)
  between operations  20 us (2%)
    convert_element_type x20, local copies, waits for them, and re-layouts, one_slab(): expanded = (picked.astype(jnp.float32)[:, :, :, None, :] * spread[None, N...  310 us
    convert_element_type x20, other arithmetic, one_slab(): expanded = (picked.astype(jnp.float32)[:, :, :, None, :] * spread[None, N...  189 us
    dot_general x20, matrix products, one_slab(): jnp.einsum('bil,bcln->cbin', weights, expanded, preferred_element_type=jn...  142 us
    all_gather x1, waiting for transfers between devices, apply_jacobian(): lax.all_gather(triple_blocks, 'elem', axis=2, tiled=True)  62.9 us
    all_to_all x2, waiting for transfers between devices, apply_jacobian(): lax.all_to_all(jnp.stack([gradients] * lax.axis_size('mode')), 'mode', 0, 0)  53.8 us
    unnamed x214, local copies, waits for them, and re-layouts  26.6 us
    all_gather x1, blocking collectives, per_device(): lax.all_gather(node_terms.T.astype(jnp.bfloat16), 'mode', axis=1, tiled=T...  22.8 us
  transfers between devices with their start and end apart: 8, of which 3 were waited for; matrix products, arithmetic and copies ran while one was open for 13% of the time, Pallas kernels for 0%

profile of v1, /device:TPU:34, one launch (start us, length us, event | category | flops | bytes accessed | tf_op | source)
XLA Modules:
  0.0 1058.3 jit_solution(16838757615371968246)
XLA Ops:
  49.7 29.6 %all-to-all-done = bf16[8,3,60,1024]{3,2,1,0:T(8,128)(2,1)} async-done(((bf16[8,3,60,1024]{3,2,1,0:T(8,128)(2,1)}), bf16[8,3,60,1024]{3,2,1,0:T(8,128)(2,1)}, u32[]{:S(2)}, u32[]{:S(2)}) %all-to-all-start) | async-done | bytes 2949152 | tf_op jit(solution)/shard_map/all_to_all | solution.py:173
  91.1 62.9 %all-gather.2.cloned.1.call-done = bf16[1,60,20160]{1,0,2:T(2,128)(2,1)} async-done(((bf16[1,60,1260]{1,0,2:T(2,128)(2,1)}), bf16[1,60,20160]{1,0,2:T(2,128)(2,1)}) %all-gather.2.cloned.1.call-update) | async-done | bytes 2419216 | tf_op jit(solution)/shard_map/all_gather | solution.py:179
  154.0 20.8 %copy.454 = bf16[1,60,20160]{2,1,0:T(8,128)(2,1)} copy(bf16[1,60,20160]{1,0,2:T(2,128)(2,1)} %all-gather.2.cloned.1.call-done) | data formatting | bytes 4838400
  176.3 22.8 %all_gather.7 = bf16[84,1024]{1,0:T(8,128)(2,1)S(1)} all-gather(bf16[84,128]{1,0:T(8,128)(2,1)S(1)} %fusion.9), channel_id=1, replica_groups=mesh['elem'=16,'mode'=8] {'mode'}, dimensions={1}, use_global_device_ids=true | all-gather | bytes 193536 | tf_op jit(solution)/shard_map/all_gather | solution.py:237
  199.2 330.1 %while.32 = (s32[]{:T(128)}, f32[3,1,60,1024]{3,2,0,1:T(8,128)S(1)}, bf16[1,3,240,1024]{3,2,1,0:T(8,128)(2,1)}, f32[84,1024]{1,0:T(8,128)S(1)}, bf16[1,60,20160]...) while((s32[]{:T(128)}, ...), condition=%wide.region_2.3_spmd.clone, body=%wide.region_1.2_spmd.clone.sunk | while | flops 756006912 | bytes 52363480 | solution.py:162
  200.2 9.4 multiply_convert_fusion.4
  209.6 15.5 %convert_element_type.118 = bf16[3,2016,1024]{2,1,0:T(8,128)(2,1)} reshape(bf16[3,24,84,1024]{3,2,1,0:T(8,128)(2,1)} %multiply_convert_fusion.4) | data formatting | bytes 24772608 | tf_op jit(solution)/shard_map/while/body/eval_jaxpr/convert_element_type | solution.py:155
  233.2 9.4 multiply_convert_fusion.4
  242.6 15.5 %convert_element_type.118 = bf16[3,2016,1024]{2,1,0:T(8,128)(2,1)} reshape(bf16[3,24,84,1024]{3,2,1,0:T(8,128)(2,1)} %multiply_convert_fusion.4) | data formatting | bytes 24772608 | tf_op jit(solution)/shard_map/while/body/eval_jaxpr/convert_element_type | solution.py:155
  266.2 9.4 multiply_convert_fusion.4
  275.6 15.5 %convert_element_type.118 = bf16[3,2016,1024]{2,1,0:T(8,128)(2,1)} reshape(bf16[3,24,84,1024]{3,2,1,0:T(8,128)(2,1)} %multiply_convert_fusion.4) | data formatting | bytes 24772608 | tf_op jit(solution)/shard_map/while/body/eval_jaxpr/convert_element_type | solution.py:155
  299.2 9.4 multiply_convert_fusion.4
  308.6 15.5 %convert_element_type.118 = bf16[3,2016,1024]{2,1,0:T(8,128)(2,1)} reshape(bf16[3,24,84,1024]{3,2,1,0:T(8,128)(2,1)} %multiply_convert_fusion.4) | data formatting | bytes 24772608 | tf_op jit(solution)/shard_map/while/body/eval_jaxpr/convert_element_type | solution.py:155
  332.2 9.4 multiply_convert_fusion.4
  341.6 15.5 %convert_element_type.118 = bf16[3,2016,1024]{2,1,0:T(8,128)(2,1)} reshape(bf16[3,24,84,1024]{3,2,1,0:T(8,128)(2,1)} %multiply_convert_fusion.4) | data formatting | bytes 24772608 | tf_op jit(solution)/shard_map/while/body/eval_jaxpr/convert_element_type | solution.py:155
  365.2 9.4 multiply_convert_fusion.4
  374.6 15.5 %convert_element_type.118 = bf16[3,2016,1024]{2,1,0:T(8,128)(2,1)} reshape(bf16[3,24,84,1024]{3,2,1,0:T(8,128)(2,1)} %multiply_convert_fusion.4) | data formatting | bytes 24772608 | tf_op jit(solution)/shard_map/while/body/eval_jaxpr/convert_element_type | solution.py:155
  398.2 9.4 multiply_convert_fusion.4
  407.6 15.5 %convert_element_type.118 = bf16[3,2016,1024]{2,1,0:T(8,128)(2,1)} reshape(bf16[3,24,84,1024]{3,2,1,0:T(8,128)(2,1)} %multiply_convert_fusion.4) | data formatting | bytes 24772608 | tf_op jit(solution)/shard_map/while/body/eval_jaxpr/convert_element_type | solution.py:155
  431.2 9.4 multiply_convert_fusion.4
  440.6 15.5 %convert_element_type.118 = bf16[3,2016,1024]{2,1,0:T(8,128)(2,1)} reshape(bf16[3,24,84,1024]{3,2,1,0:T(8,128)(2,1)} %multiply_convert_fusion.4) | data formatting | bytes 24772608 | tf_op jit(solution)/shard_map/while/body/eval_jaxpr/convert_element_type | solution.py:155
  464.2 9.4 multiply_convert_fusion.4
  473.6 15.5 %convert_element_type.118 = bf16[3,2016,1024]{2,1,0:T(8,128)(2,1)} reshape(bf16[3,24,84,1024]{3,2,1,0:T(8,128)(2,1)} %multiply_convert_fusion.4) | data formatting | bytes 24772608 | tf_op jit(solution)/shard_map/while/body/eval_jaxpr/convert_element_type | solution.py:155
  497.2 9.4 multiply_convert_fusion.4
  506.7 15.5 %convert_element_type.118 = bf16[3,2016,1024]{2,1,0:T(8,128)(2,1)} reshape(bf16[3,24,84,1024]{3,2,1,0:T(8,128)(2,1)} %multiply_convert_fusion.4) | data formatting | bytes 24772608 | tf_op jit(solution)/shard_map/while/body/eval_jaxpr/convert_element_type | solution.py:155
  595.2 8.1 all-to-all-start.1
  621.9 24.2 %all-to-all-done.1 = bf16[8,3,60,1024]{3,2,1,0:T(8,128)(2,1)} async-done(((bf16[8,3,60,1024]{3,2,1,0:T(8,128)(2,1)}), bf16[8,3,60,1024]{3,2,1,0:T(8,128)(2,1)}, u32[]{:S(2)}, u32[]{:S(2)}) %all-to-all-start.1) | async-done | bytes 2949152 | tf_op jit(solution)/shard_map/all_to_all | solution.py:173
  657.9 330.1 %while.33 = (s32[]{:T(128)}, f32[3,1,60,1024]{3,2,0,1:T(8,128)S(1)}, bf16[1,3,240,1024]{3,2,1,0:T(8,128)(2,1)}, f32[84,1024]{1,0:T(8,128)S(1)}, bf16[1,60,20160]...) while((s32[]{:T(128)}, ...), condition=%wide.region_4.6_spmd.clone, body=%wide.region_3.5_spmd.clone.sunk | while | flops 756006912 | bytes 52363480 | solution.py:162
  658.8 9.4 multiply_convert_fusion.5
  668.2 15.5 %convert_element_type.120 = bf16[3,2016,1024]{2,1,0:T(8,128)(2,1)} reshape(bf16[3,24,84,1024]{3,2,1,0:T(8,128)(2,1)} %multiply_convert_fusion.5) | data formatting | bytes 24772608 | tf_op jit(solution)/shard_map/while/body/eval_jaxpr/convert_element_type | solution.py:155
  691.8 9.4 multiply_convert_fusion.5
  701.3 15.5 %convert_element_type.120 = bf16[3,2016,1024]{2,1,0:T(8,128)(2,1)} reshape(bf16[3,24,84,1024]{3,2,1,0:T(8,128)(2,1)} %multiply_convert_fusion.5) | data formatting | bytes 24772608 | tf_op jit(solution)/shard_map/while/body/eval_jaxpr/convert_element_type | solution.py:155
  724.8 9.4 multiply_convert_fusion.5
  734.3 15.5 %convert_element_type.120 = bf16[3,2016,1024]{2,1,0:T(8,128)(2,1)} reshape(bf16[3,24,84,1024]{3,2,1,0:T(8,128)(2,1)} %multiply_convert_fusion.5) | data formatting | bytes 24772608 | tf_op jit(solution)/shard_map/while/body/eval_jaxpr/convert_element_type | solution.py:155
  757.8 9.4 multiply_convert_fusion.5
  767.2 15.5 %convert_element_type.120 = bf16[3,2016,1024]{2,1,0:T(8,128)(2,1)} reshape(bf16[3,24,84,1024]{3,2,1,0:T(8,128)(2,1)} %multiply_convert_fusion.5) | data formatting | bytes 24772608 | tf_op jit(solution)/shard_map/while/body/eval_jaxpr/convert_element_type | solution.py:155
  790.8 9.4 multiply_convert_fusion.5
  800.3 15.5 %convert_element_type.120 = bf16[3,2016,1024]{2,1,0:T(8,128)(2,1)} reshape(bf16[3,24,84,1024]{3,2,1,0:T(8,128)(2,1)} %multiply_convert_fusion.5) | data formatting | bytes 24772608 | tf_op jit(solution)/shard_map/while/body/eval_jaxpr/convert_element_type | solution.py:155
  823.8 9.4 multiply_convert_fusion.5
  833.3 15.5 %convert_element_type.120 = bf16[3,2016,1024]{2,1,0:T(8,128)(2,1)} reshape(bf16[3,24,84,1024]{3,2,1,0:T(8,128)(2,1)} %multiply_convert_fusion.5) | data formatting | bytes 24772608 | tf_op jit(solution)/shard_map/while/body/eval_jaxpr/convert_element_type | solution.py:155
  856.8 9.4 multiply_convert_fusion.5
  866.3 15.5 %convert_element_type.120 = bf16[3,2016,1024]{2,1,0:T(8,128)(2,1)} reshape(bf16[3,24,84,1024]{3,2,1,0:T(8,128)(2,1)} %multiply_convert_fusion.5) | data formatting | bytes 24772608 | tf_op jit(solution)/shard_map/while/body/eval_jaxpr/convert_element_type | solution.py:155
  889.8 9.4 multiply_convert_fusion.5
  899.3 15.5 %convert_element_type.120 = bf16[3,2016,1024]{2,1,0:T(8,128)(2,1)} reshape(bf16[3,24,84,1024]{3,2,1,0:T(8,128)(2,1)} %multiply_convert_fusion.5) | data formatting | bytes 24772608 | tf_op jit(solution)/shard_map/while/body/eval_jaxpr/convert_element_type | solution.py:155
  922.8 9.4 multiply_convert_fusion.5
  932.3 15.5 %convert_element_type.120 = bf16[3,2016,1024]{2,1,0:T(8,128)(2,1)} reshape(bf16[3,24,84,1024]{3,2,1,0:T(8,128)(2,1)} %multiply_convert_fusion.5) | data formatting | bytes 24772608 | tf_op jit(solution)/shard_map/while/body/eval_jaxpr/convert_element_type | solution.py:155
  955.8 9.4 multiply_convert_fusion.5
  965.3 15.5 %convert_element_type.120 = bf16[3,2016,1024]{2,1,0:T(8,128)(2,1)} reshape(bf16[3,24,84,1024]{3,2,1,0:T(8,128)(2,1)} %multiply_convert_fusion.5) | data formatting | bytes 24772608 | tf_op jit(solution)/shard_map/while/body/eval_jaxpr/convert_element_type | solution.py:155
  (481 shorter events, 370.6 us)
Async XLA Ops:
  8.0 146.0 %all-gather.2.cloned.1.call-start = ((), (), s32[]{:S(2)}) async-start(), calls=%async_computation.4 | async-start | bytes 10967040 | tf_op jit(solution)/shard_map/all_gather | solution.py:179
  10.2 164.7 %reduce-scatter.2.cloned.1.call-start = ((), (), s32[]{:S(2)}) async-start(), calls=%async_computation.3 | async-start | bytes 4718592 | tf_op jit(solution)/shard_map/reduce_scatter | solution.py:226
  20.4 58.9 %all-to-all-start = ((bf16[8,3,60,1024]{3,2,1,0:T(8,128)(2,1)}), bf16[8,3,60,1024]{3,2,1,0:T(8,128)(2,1)}, u32[]{:S(2)}, u32[]{:S(2)}) async-start(bf16[8,3,60,1024]{3,2,1,0:T(8,128)(2,1)} %stack.92), calls=%async_computation | async-start | bytes 6291456 | tf_op jit(solution)/shard_map/all_to_all | solution.py:173
  33.1 498.2 %copy-start.81 = (s32[1024]{0:T(1024)}, s32[1024]{0:T(1024)S(1)}, u32[]{:S(2)}) copy-start(s32[1024]{0:T(1024)S(1)} %pad_clamp_fusion.3) | copy-start | bytes 12292
  35.5 497.9 %copy-start.80 = (s32[1024]{0:T(1024)}, s32[1024]{0:T(1024)S(1)}, u32[]{:S(2)}) copy-start(s32[1024]{0:T(1024)S(1)} %pad_clamp_fusion.5) | copy-start | bytes 12292
  36.3 7.0 copy-start
  36.4 497.6 %copy-start.83 = (s32[1024]{0:T(1024)}, s32[1024]{0:T(1024)S(1)}, u32[]{:S(2)}) copy-start(s32[1024]{0:T(1024)S(1)} %pad_clamp_fusion.7) | copy-start | bytes 12292
  39.7 499.4 %copy-start.84 = (s32[1024]{0:T(1024)}, s32[1024]{0:T(1024)S(1)}, u32[]{:S(2)}) copy-start(s32[1024]{0:T(1024)S(1)} %pad_clamp_fusion.11) | copy-start | bytes 12292
  42.0 527.0 %copy-start.93 = (pred[16]{0:T(512)(128)(4,1)}, pred[16]{0:T(512)(128)(4,1)S(1)}, u32[]{:S(2)}) copy-start(pred[16]{0:T(512)(128)(4,1)S(1)} %get-tuple-element.439) | copy-start | bytes 52
  42.0 528.0 %copy-start.95 = (pred[16]{0:T(512)(128)(4,1)}, pred[16]{0:T(512)(128)(4,1)S(1)}, u32[]{:S(2)}) copy-start(pred[16]{0:T(512)(128)(4,1)S(1)} %get-tuple-element.441) | copy-start | bytes 52
  42.0 538.5 %copy-start.89 = (pred[16]{0:T(512)(128)(4,1)}, pred[16]{0:T(512)(128)(4,1)S(1)}, u32[]{:S(2)}) copy-start(pred[16]{0:T(512)(128)(4,1)S(1)} %get-tuple-element.395) | copy-start | bytes 52
  42.0 541.1 %copy-start.91 = (pred[16]{0:T(512)(128)(4,1)}, pred[16]{0:T(512)(128)(4,1)S(1)}, u32[]{:S(2)}) copy-start(pred[16]{0:T(512)(128)(4,1)S(1)} %get-tuple-element.443) | copy-start | bytes 52
  42.0 503.8 %copy-start.86 = (s32[1024]{0:T(1024)}, s32[1024]{0:T(1024)S(1)}, u32[]{:S(2)}) copy-start(s32[1024]{0:T(1024)S(1)} %pad_clamp_fusion.4) | copy-start | bytes 12292
  43.4 504.1 %copy-start.85 = (s32[1024]{0:T(1024)}, s32[1024]{0:T(1024)S(1)}, u32[]{:S(2)}) copy-start(s32[1024]{0:T(1024)S(1)} %pad_clamp_fusion.6) | copy-start | bytes 12292
  45.8 504.1 %copy-start.82 = (s32[1024]{0:T(1024)}, s32[1024]{0:T(1024)S(1)}, u32[]{:S(2)}) copy-start(s32[1024]{0:T(1024)S(1)} %pad_clamp_fusion.8) | copy-start | bytes 12292
  47.2 504.4 %copy-start.87 = (s32[1024]{0:T(1024)}, s32[1024]{0:T(1024)S(1)}, u32[]{:S(2)}) copy-start(s32[1024]{0:T(1024)S(1)} %pad_clamp_fusion.10) | copy-start | bytes 12292
  534.5 7.7 copy-start.71
  536.4 7.6 copy-start.70
  541.1 8.6 copy-start.23
  542.9 29.1 %collective-permute-start.1 = (f32[1,2,60,256]{2,3,1,0:T(8,128)}, f32[1,2,60,256]{2,3,1,0:T(8,128)}, u32[]{:S(2)}, u32[]{:S(2)}) collective-permute-start(f32[1,2,60,256]{2,3,1,0:T(8,128)} %pad_maximum_fusion.3), channel_id=1, source_target_pairs={{8,0},{16,8},{24,16},{32,24},{40,32},{48,40},{56,48},{64,56},{72,6... | collective-permute-start | bytes 368648 | tf_op jit(solution)/shard_map/ppermute | solution.py:32
  544.0 7.3 copy-start.22
  544.8 31.5 %collective-permute-start = (f32[1,2,60,256]{2,3,1,0:T(8,128)}, f32[1,2,60,256]{2,3,1,0:T(8,128)}, u32[]{:S(2)}, u32[]{:S(2)}) collective-permute-start(f32[1,2,60,256]{2,3,1,0:T(8,128)} %pad_maximum_fusion.2), channel_id=1, source_target_pairs={{0,8},{8,16},{16,24},{24,32},{32,40},{40,48},{48,56},{56,64},{64,7... | collective-permute-start | bytes 368648 | tf_op jit(solution)/shard_map/ppermute | solution.py:29
  545.8 8.9 copy-start.68
  547.5 12.4 %copy-start.64 = (f32[128,128]{1,0:T(8,128)S(1)}, f32[128,128]{1,0:T(8,128)}, u32[]{:S(2)}) copy-start(f32[128,128]{1,0:T(8,128)} %constant.210.clone) | copy-start | bytes 196612
  549.6 14.5 %copy-start.4 = (f32[16,60,16]{0,1,2:T(8,128)S(1)}, f32[16,60,16]{0,1,2:T(8,128)}, u32[]{:S(2)}) copy-start(f32[16,60,16]{0,1,2:T(8,128)} %copy.468) | copy-start | bytes 184324
  549.6 14.5 %copy-start.97 = (pred[16]{0:T(512)(128)(4,1)S(1)}, pred[16]{0:T(512)(128)(4,1)}, u32[]{:S(2)}) copy-start(pred[16]{0:T(512)(128)(4,1)} %get-tuple-element.435) | copy-start | bytes 52
  551.6 8.2 copy-start.10
  551.6 11.8 %copy-start.74 = (bf16[1,1,60,1024]{3,2,0,1:T(8,128)(2,1)S(1)}, bf16[1,1,60,1024]{3,2,0,1:T(8,128)(2,1)}, u32[]{:S(2)}) copy-start(bf16[1,1,60,1024]{3,2,0,1:T(8,128)(2,1)} %get-tuple-element.422) | copy-start | bytes 368644
  551.6 15.1 %copy-start.1 = (f32[16,60,16]{0,1,2:T(8,128)S(1)}, f32[16,60,16]{0,1,2:T(8,128)}, u32[]{:S(2)}) copy-start(f32[16,60,16]{0,1,2:T(8,128)} %copy-done) | copy-start | bytes 184324
  551.6 15.1 %copy-start.99 = (pred[16]{0:T(512)(128)(4,1)S(1)}, pred[16]{0:T(512)(128)(4,1)}, u32[]{:S(2)}) copy-start(pred[16]{0:T(512)(128)(4,1)} %get-tuple-element.437) | copy-start | bytes 52
  561.7 7.3 copy-start.5
  595.2 8.1 copy-start.51
  595.2 51.0 %all-to-all-start.1 = ((bf16[8,3,60,1024]{3,2,1,0:T(8,128)(2,1)}), bf16[8,3,60,1024]{3,2,1,0:T(8,128)(2,1)}, u32[]{:S(2)}, u32[]{:S(2)}) async-start(bf16[8,3,60,1024]{3,2,1,0:T(8,128)(2,1)} %stack.104), calls=%async_computation.2 | async-start | bytes 6291456 | tf_op jit(solution)/shard_map/all_to_all | solution.py:173
  610.4 7.9 copy-start.25
  612.2 7.9 copy-start.24
  614.2 7.7 copy-start.13
  992.5 7.8 copy-start.73
  994.4 7.7 copy-start.72
  999.1 13.7 %copy-start.21 = (f32[16,60,16]{1,2,0:T(8,128)S(1)}, f32[16,60,16]{1,2,0:T(8,128)}, u32[]{:S(2)}) copy-start(f32[16,60,16]{1,2,0:T(8,128)} %gather_fusion.12) | copy-start | bytes 184324
  1000.9 32.0 %collective-permute-start.2 = (f32[1,2,60,256]{2,3,1,0:T(8,128)}, f32[1,2,60,256]{2,3,1,0:T(8,128)}, u32[]{:S(2)}, u32[]{:S(2)}) collective-permute-start(f32[1,2,60,256]{2,3,1,0:T(8,128)} %pad_maximum_fusion.4), channel_id=1, source_target_pairs={{0,8},{8,16},{16,24},{24,32},{32,40},{40,48},{48,56},{56,64},{64,7... | collective-permute-start | bytes 368648 | tf_op jit(solution)/shard_map/ppermute | solution.py:29
  1002.0 12.7 %copy-start.20 = (f32[16,60,16]{1,2,0:T(8,128)S(1)}, f32[16,60,16]{1,2,0:T(8,128)}, u32[]{:S(2)}) copy-start(f32[16,60,16]{1,2,0:T(8,128)} %gather_fusion.13) | copy-start | bytes 184324
  1002.8 34.5 %collective-permute-start.3 = (f32[1,2,60,256]{2,3,1,0:T(8,128)}, f32[1,2,60,256]{2,3,1,0:T(8,128)}, u32[]{:S(2)}, u32[]{:S(2)}) collective-permute-start(f32[1,2,60,256]{2,3,1,0:T(8,128)} %pad_maximum_fusion.5), channel_id=1, source_target_pairs={{8,0},{16,8},{24,16},{32,24},{40,32},{48,40},{56,48},{64,56},{72,6... | collective-permute-start | bytes 368648 | tf_op jit(solution)/shard_map/ppermute | solution.py:32
  1008.6 11.4 %copy-start.69 = (f32[128,128]{1,0:T(8,128)S(1)}, f32[128,128]{1,0:T(8,128)}, u32[]{:S(2)}) copy-start(f32[128,128]{1,0:T(8,128)} %constant.209.clone) | copy-start | bytes 196612
  1010.5 13.0 %copy-start.66 = (f32[128,128]{1,0:T(8,128)S(1)}, f32[128,128]{1,0:T(8,128)}, u32[]{:S(2)}) copy-start(f32[128,128]{1,0:T(8,128)} %constant.210.clone) | copy-start | bytes 196612
  1012.8 14.3 %copy-start.14 = (f32[16,60,16]{0,1,2:T(8,128)S(1)}, f32[16,60,16]{0,1,2:T(8,128)}, u32[]{:S(2)}) copy-start(f32[16,60,16]{0,1,2:T(8,128)} %copy-done.13) | copy-start | bytes 184324
  1012.8 14.3 %copy-start.16 = (f32[16,60,16]{0,1,2:T(8,128)S(1)}, f32[16,60,16]{0,1,2:T(8,128)}, u32[]{:S(2)}) copy-start(f32[16,60,16]{0,1,2:T(8,128)} %copy-done.15) | copy-start | bytes 184324
  1012.8 14.3 %copy-start.98 = (pred[16]{0:T(512)(128)(4,1)S(1)}, pred[16]{0:T(512)(128)(4,1)}, u32[]{:S(2)}) copy-start(pred[16]{0:T(512)(128)(4,1)} %get-tuple-element.435) | copy-start | bytes 52
  1012.8 14.3 %copy-start.100 = (pred[16]{0:T(512)(128)(4,1)S(1)}, pred[16]{0:T(512)(128)(4,1)}, u32[]{:S(2)}) copy-start(pred[16]{0:T(512)(128)(4,1)} %get-tuple-element.437) | copy-start | bytes 52
  (66 other events, 225.2 us)
Sparse Core Ops, SparseCore 0:
  11.3 142.6 all-gather.1
Sparse Core Ops, SparseCore 1:
  14.1 159.3 reduce-scatter.1
